TPU v7x, 512 devices: a whole 4x8x8 slice. The times are simulated.
512 devices in a mesh: band: 64 (over z_lo, y, core), strip: 8 (over z_hi, x).
Axes of the slice: x: 4, y: 8, z: 8 (z_hi: 2, z_lo: 4; z = z_hi * 4 + z_lo), core: 2. Of those that a mesh axis runs over, the one named last changes fastest.
Arguments:
- activations: bfloat16 [64, 320, 48, 128], P('band', None, 'strip'), may hold values from -16 to 16
- out_grad: bfloat16 [64, 320, 48, 128], P('band', None, 'strip'), may hold values from -6 to 6
- kernel: bfloat16 [320, 9, 320], P('band', None, 'strip'), may hold values from -0.109375 to 0.109375
Outputs:
- input_grad: bfloat16 [64, 320, 48, 128], P('band', None, 'strip')
- kernel_grad: float32 [320, 9, 320], P('band', None, 'strip')
All inputs are finite; a program needn't handle non-finite values.
Results may differ from a plain program's by a relative error of at most 0.001.
Values may be sent and summed in bfloat16 or wider, within the bound.
A program may use at most 64 MiB of HBM per device.

v0:
```python
import math
import jax
import jax.numpy as jnp
from jax import lax
from jax.sharding import PartitionSpec as P

OFFSETS = ((-1, -1), (-1, 0), (-1, 1), (0, -1), (0, 0), (0, 1), (1, -1), (1, 0), (1, 1))


def extended(cells, sides, width):
    for axis, dim in sides:
        count = lax.axis_size(axis)
        ends = count - 1
        head = lax.slice_in_dim(cells, 0, width, axis=dim)
        tail = lax.slice_in_dim(cells, cells.shape[dim] - width, cells.shape[dim], axis=dim)
        cells = jnp.concatenate(
            [
                lax.ppermute(tail, axis, [(i, (i + 1) % count) for i in range(ends)]),
                cells,
                lax.ppermute(head, axis, [((i + 1) % count, i) for i in range(ends)]),
            ],
            axis=dim,
        )
    return cells


def tap_slice(field, row_step, col_step):
    row_count = field.shape[2] - 2
    col_count = field.shape[3] - 2
    return field[
        :, :, 1 + row_step : 1 + row_step + row_count, 1 + col_step : 1 + col_step + col_count
    ]


def body(activations, out_grad, kernel):
    images = activations.shape[0]
    row_count = activations.shape[2]
    col_count = activations.shape[3]
    cell_total = images * lax.axis_size("band") * row_count * lax.axis_size("strip") * col_count
    grad_scale = 1.0 / math.sqrt(cell_total)
    grad_padded = extended(out_grad, (("strip", 2),), 1)
    grad_padded = jnp.pad(grad_padded, ((0, 0), (0, 0), (0, 0), (1, 1)))
    kernel_full_cols = lax.all_gather(kernel, "strip", axis=2, tiled=True)
    kernel_whole = lax.all_gather(kernel_full_cols, "band", axis=0, tiled=True)
    summed = jnp.zeros((images, kernel_whole.shape[0], row_count, col_count), jnp.float32)
    for tap_index, (row_step, col_step) in enumerate(OFFSETS):
        shifted = tap_slice(grad_padded, -row_step, -col_step)
        summed = summed + jnp.einsum(
            "io,bohw->bihw",
            kernel_whole[:, tap_index, :],
            shifted,
            preferred_element_type=jnp.float32,
        )
    input_grad = summed.astype(jnp.bfloat16)
    blocks = []
    for tap_index, (row_step, col_step) in enumerate(OFFSETS):
        grad_side = tap_slice(grad_padded, -row_step, -col_step)
        blocks.append(
            jnp.einsum("bihw,bohw->io", activations, grad_side, preferred_element_type=jnp.float32)
        )
    partial_value = lax.psum_scatter(
        jnp.stack(blocks, axis=1), "band", scatter_dimension=0, tiled=True
    )
    kernel_sum = lax.psum_scatter(partial_value, "strip", scatter_dimension=2, tiled=True)
    return (input_grad, kernel_sum * grad_scale)


def solution(mesh):
    in_specs = (
        P("band", None, "strip", None),
        P("band", None, "strip", None),
        P("band", None, "strip"),
    )
    out_specs = (P("band", None, "strip", None), P("band", None, "strip"))
    return jax.shard_map(body, mesh=mesh, in_specs=in_specs, out_specs=out_specs, check_vma=False)
```

profile of v0, /device:TPU:4, one launch (start us, length us, event | category | flops | bytes accessed | tf_op | source)
XLA Modules:
  0.0 532.6 jit_solution(4342535424170789729)
XLA Ops:
  7.2 0.0 copy-start
  7.2 0.0 all-gather.2.cloned.1.call-start
  7.2 0.9 copy.21
  8.1 0.0 copy-start.1
  8.2 48.1 %all_gather.6 = bf16[5,9,320]{1,0,2:T(8,128)(2,1)S(1)} all-gather(bf16[5,9,40]{1,0,2:T(8,128)(2,1)S(1)} %copy.21), channel_id=1, replica_groups=mesh['band'=64,'strip'=8] {'strip'}, dimensions={2}, use_global_device_ids=true | all-gather | bytes 32400 | tf_op jit(solution)/shard_map/all_gather | solution.py:43
  56.3 1.0 copy.22
  57.3 0.0 all-gather.2.cloned.1.call-update
  57.3 0.0 reduce-scatter.3.cloned.1.call-start
  57.3 0.9 fusion.42
  58.3 3.0 collective-permute-start.1
  61.3 2.8 collective-permute-start
  64.1 0.5 collective-permute-done.1
  64.6 3.3 collective-permute-done
  68.0 1.7 fusion.6
  69.7 0.0 copy-done
  69.7 1.3 fusion.17
  71.0 0.0 copy-done.1
  71.0 1.3 fusion.16
  72.2 1.3 fusion.15
  73.5 1.3 fusion.14
  74.8 1.2 fusion.13
  76.0 1.3 fusion.12
  77.2 1.3 fusion.11
  78.5 1.2 fusion.10
  79.7 1.2 fusion.9
  81.0 9.0 %copy.33 = f32[320,9,320]{2,1,0:T(8,128)} copy(f32[320,9,320]{0,2,1:T(8,128)} %fusion.9) | data formatting | bytes 7372800 | tf_op jit(solution)/shard_map/stack | solution.py:62
  89.9 0.0 reduce-scatter.3.cloned.1.call-update
  90.0 1.3 dynamic-slice
  91.9 87.8 %all-gather.2.cloned.1.call-done = bf16[320,9,320]{2,1,0:T(8,128)(2,1)} async-done(((bf16[5,9,320]{2,1,0:T(8,128)(2,1)}), bf16[320,9,320]{2,1,0:T(8,128)(2,1)}) %all-gather.2.cloned.1.call-update) | async-done | bytes 1843216 | tf_op jit(solution)/shard_map/all_gather | solution.py:44
  179.7 10.5 %fusion.41 = (bf16[320,1,320]{2,1,0:T(2,128)(2,1)S(1)}, bf16[320,1,320]{2,1,0:T(2,128)(2,1)S(1)}, bf16[320,1,320]{2,1,0:T(2,128)(2,1)S(1)}, bf16[320,1,320]{2,1,...) fusion(bf16[320,9,320]{2,1,0:T(8,128)(2,1)} %all-gather.2.clone, ...), kind=kLoop, calls=%fused_computation.73 | loop fusion | bytes 3686400 | tf_op jit(solution)/shard_map/slice | solution.py:50
  190.3 0.4 fusion.32
  190.7 0.5 fusion.31
  191.2 0.4 convolution_add_fusion.6
  191.6 0.4 convolution_add_fusion.5
  192.0 0.5 convolution_add_fusion.4
  192.5 0.4 convolution_add_fusion.3
  193.0 0.4 convolution_add_fusion.2
  193.4 0.5 convolution_add_fusion.1
  193.9 1.2 fusion.8
  195.1 280.4 %reduce-scatter.3.cloned.1.call-done = f32[5,9,320]{2,1,0:T(8,128)} async-done(((f32[320,9,320]{2,1,0:T(8,128)}), f32[5,9,320]{2,1,0:T(8,128)}) %reduce-scatter.3.cloned.1.call-update) | async-done | bytes 57616 | tf_op jit(solution)/shard_map/reduce_scatter | solution.py:61
  475.5 49.6 %all-reduce.1 = f32[5,9,320]{2,1,0:T(8,128)S(1)} all-reduce(f32[5,9,320]{2,1,0:T(8,128)} %reduce-scatter.3.cloned.1.call-done), channel_id=3, replica_groups=mesh['band'=64,'strip'=8] {'strip'}, use_global_device_ids=true, to_apply=%region_1.2.clone | all-reduce | flops 14400 | bytes 115200
  525.1 0.1 dynamic-slice_multiply_fusion
  525.2 0.6 copy.34
Async XLA Ops:
  7.2 62.5 %copy-start = (bf16[1,320,6,128]{3,1,2,0:T(8,128)(2,1)S(1)}, bf16[1,320,6,128]{3,1,2,0:T(8,128)(2,1)}, u32[]{:S(2)}) copy-start(bf16[1,320,6,128]{3,1,2,0:T(8,128)(2,1)} %param.3) | copy-start | bytes 1474564
  7.2 172.5 %all-gather.2.cloned.1.call-start = ((), (), s32[]{:S(2)}) async-start(), calls=%async_computation.1 | async-start | bytes 3993600 | tf_op jit(solution)/shard_map/all_gather | solution.py:44
  8.1 62.8 %copy-start.1 = (bf16[1,320,6,128]{3,1,2,0:T(8,128)(2,1)S(1)}, bf16[1,320,6,128]{3,1,2,0:T(8,128)(2,1)}, u32[]{:S(2)}) copy-start(bf16[1,320,6,128]{3,1,2,0:T(8,128)(2,1)} %param.4) | copy-start | bytes 1474564
  57.3 418.2 %reduce-scatter.3.cloned.1.call-start = ((), (), s32[]{:S(2)}) async-start(), calls=%async_computation.2 | async-start | bytes 7987200 | tf_op jit(solution)/shard_map/reduce_scatter | solution.py:61
  58.3 6.3 %collective-permute-start.1 = (bf16[1,320,1,128]{3,1,2,0:T(8,128)(2,1)S(1)}, bf16[1,320,1,128]{3,1,2,0:T(8,128)(2,1)S(1)}, u32[]{:S(2)}, u32[]{:S(2)}) collective-permute-start(bf16[1,320,1,128]{3,1,2,0:T(8,128)(2,1)S(1)} %get-tuple-element.18), channel_id=1, source_target_pairs={{1,0},{2,1},{3,2},{4,3},{5,4},{6,5},{7,6},{9,8},{10,9},{11,10},{12... | collective-permute-start | bytes 245768 | tf_op jit(solution)/shard_map/ppermute | solution.py:20
  61.3 6.6 %collective-permute-start = (bf16[1,320,1,128]{3,1,2,0:T(8,128)(2,1)S(1)}, bf16[1,320,1,128]{3,1,2,0:T(8,128)(2,1)S(1)}, u32[]{:S(2)}, u32[]{:S(2)}) collective-permute-start(bf16[1,320,1,128]{3,1,2,0:T(8,128)(2,1)S(1)} %get-tuple-element.17), channel_id=1, source_target_pairs={{0,1},{1,2},{2,3},{3,4},{4,5},{5,6},{6,7},{8,9},{9,10},{10,11},{11... | collective-permute-start | bytes 245768 | tf_op jit(solution)/shard_map/ppermute | solution.py:18
Sparse Core Ops, SparseCore 0:
  57.4 122.2 all-gather.1
  182.6 292.8 reduce-scatter.2
where the time goes:
time: 533 us
  waiting for transfers between devices  372 us (70%)
  blocking collectives  97.7 us (18%)
  local copies, waits for them, and re-layouts  24.3 us (5%)
  matrix products  16.1 us (3%)
  between operations  14.8 us (3%)
  starting transfers between devices  5.92 us (1%)
    reduce_scatter x1, waiting for transfers between devices, body(): lax.psum_scatter(jnp.stack(blocks, axis=1), 'band', scatter_dimension=0,...  280 us
    all_gather x1, waiting for transfers between devices, body(): kernel_whole = lax.all_gather(kernel_full_cols, 'band', axis=0, tiled=True)  87.8 us
    unnamed x1, blocking collectives  49.6 us
    all_gather x1, blocking collectives, body(): kernel_full_cols = lax.all_gather(kernel, 'strip', axis=2, tiled=True)  48.1 us
    dot_general x9, matrix products, body(): jnp.einsum('bihw,bohw->io', activations, grad_side, preferred_element_typ...  11.3 us
  transfers between devices with their start and end apart: 4, of which 4 were waited for; matrix products, arithmetic and copies ran while one was open for 7% of the time, Pallas kernels for 0%

commit v1 on v0

--- a/solution.py
+++ b/solution.py
@@ -1,10 +1,22 @@
+import functools
 import math
 import jax
 import jax.numpy as jnp
 from jax import lax
 from jax.sharding import PartitionSpec as P
+from jax.lax import all_to_all, axis_size
 
 OFFSETS = ((-1, -1), (-1, 0), (-1, 1), (0, -1), (0, 0), (0, 1), (1, -1), (1, 0), (1, 1))
+
+
+def choose_views_by_axis(panel, which_axis):
+    right_arr = jnp.stack(axis_size(which_axis) * [panel])
+    return jnp.concatenate(
+        all_to_all(right_arr, concat_axis=0, split_axis=0, axis_name=which_axis), axis=0
+    )
+
+
+resolve_the_sheets = functools.partial(choose_views_by_axis, which_axis="band")
 
 
 def extended(cells, sides, width):
@@ -41,7 +53,7 @@
     grad_padded = extended(out_grad, (("strip", 2),), 1)
     grad_padded = jnp.pad(grad_padded, ((0, 0), (0, 0), (0, 0), (1, 1)))
     kernel_full_cols = lax.all_gather(kernel, "strip", axis=2, tiled=True)
-    kernel_whole = lax.all_gather(kernel_full_cols, "band", axis=0, tiled=True)
+    kernel_whole = resolve_the_sheets(kernel_full_cols)
     summed = jnp.zeros((images, kernel_whole.shape[0], row_count, col_count), jnp.float32)
     for tap_index, (row_step, col_step) in enumerate(OFFSETS):
         shifted = tap_slice(grad_padded, -row_step, -col_step)

time: 533 us -> 431 us (0.81)
  the two profiles are of different devices: /device:TPU:4 before, /device:TPU:0 now
where the time goes in v1:
time: 431 us; the launch traced here: 430 us
  waiting for transfers between devices  254 us (59%)
  blocking collectives  102 us (24%)
  local copies, waits for them, and re-layouts  25.2 us (6%)
  matrix products  18.1 us (4%)
  between operations  14.8 us (3%)
  starting transfers between devices  14.3 us (3%)
    reduce_scatter x1, waiting for transfers between devices, body(): lax.psum_scatter(jnp.stack(blocks, axis=1), 'band', scatter_dimension=0,...  159 us
    all_to_all x1, waiting for transfers between devices, choose_views_by_axis(): all_to_all(right_arr, concat_axis=0, split_axis=0, axis_name=which_axis)  92.2 us
    unnamed x1, blocking collectives  54.7 us
    all_gather x1, blocking collectives, body(): kernel_full_cols = lax.all_gather(kernel, 'strip', axis=2, tiled=True)  47.2 us
    dot_general x9, matrix products, body(): jnp.einsum('bihw,bohw->io', activations, grad_side, preferred_element_typ...  11.3 us
    another operation x1, local copies, waits for them, and re-layouts, body(): jnp.stack(blocks, axis=1)  8.98 us
  transfers between devices with their start and end apart: 4, of which 4 were waited for; matrix products, arithmetic and copies ran while one was open for 5% of the time, Pallas kernels for 0%

profile of v1, /device:TPU:0, one launch (start us, length us, event | category | flops | bytes accessed | tf_op | source)
XLA Modules:
  0.0 429.8 jit_solution(18204757727240311585)
XLA Ops:
  7.2 0.0 copy-start
  7.2 0.0 copy-start.1
  7.2 0.0 reduce-scatter.3.cloned.1.call-start
  7.2 1.0 fusion.41
  8.3 1.3 collective-permute-start.1
  9.6 4.6 %collective-permute-start = (bf16[1,320,1,128]{3,1,2,0:T(8,128)(2,1)S(1)}, bf16[1,320,1,128]{3,1,2,0:T(8,128)(2,1)S(1)}, u32[]{:S(2)}, u32[]{:S(2)}) collective-permute-start(bf16[1,320,1,128]{3,1,2,0:T(8,128)(2,1)S(1)} %get-tuple-element.10), channel_id=1, source_target_pairs={{0,1},{1,2},{2,3},{3,4},{4,5},{5,6},{6,7},{8,9},{9,10},{10,11},{11... | collective-permute-start | bytes 245768 | tf_op jit(solution)/shard_map/ppermute | solution.py:30
  14.1 0.5 collective-permute-done.1
  14.6 1.6 collective-permute-done
  16.1 1.7 fusion.6
  17.8 0.0 copy-done
  17.8 1.3 fusion.17
  19.1 0.0 copy-done.1
  19.1 1.3 fusion.16
  20.4 1.3 fusion.15
  21.7 1.3 fusion.14
  23.0 1.2 fusion.13
  24.2 1.3 fusion.12
  25.4 1.3 fusion.11
  26.7 1.2 fusion.10
  27.9 1.2 fusion.9
  29.1 9.0 %copy.19 = f32[320,9,320]{2,1,0:T(8,128)} copy(f32[320,9,320]{0,2,1:T(8,128)} %fusion.9) | data formatting | bytes 7372800 | tf_op jit(solution)/shard_map/stack | solution.py:74
  38.1 0.0 copy-start.3
  38.1 0.0 reduce-scatter.3.cloned.1.call-update
  38.1 0.7 copy-done.3
  38.8 0.2 copy.15
  39.0 47.2 %all_gather.3 = bf16[5,9,320]{1,0,2:T(8,128)(2,1)S(1)} all-gather(bf16[5,9,40]{1,0,2:T(8,128)(2,1)S(1)} %copy.15), channel_id=1, replica_groups=mesh['band'=64,'strip'=8] {'strip'}, dimensions={2}, use_global_device_ids=true | all-gather | bytes 32400 | tf_op jit(solution)/shard_map/all_gather | solution.py:55
  86.2 0.5 copy.16
  86.7 2.2 stack.22
  88.8 8.5 %all-to-all-start = ((bf16[64,5,9,320]{3,1,2,0:T(8,128)(2,1)}), bf16[64,5,9,320]{3,1,2,0:T(8,128)(2,1)}, u32[]{:S(2)}, u32[]{:S(2)}) async-start(bf16[64,5,9,320]{3,1,2,0:T(8,128)(2,1)} %stack.22), calls=%async_computation | async-start | bytes 7077888 | tf_op jit(solution)/shard_map/all_to_all | solution.py:15
  97.3 1.3 dynamic-slice
  99.2 92.2 %all-to-all-done = bf16[64,5,9,320]{3,1,2,0:T(8,128)(2,1)} async-done(((bf16[64,5,9,320]{3,1,2,0:T(8,128)(2,1)}), bf16[64,5,9,320]{3,1,2,0:T(8,128)(2,1)}, u32[]{:S(2)}, u32[]{:S(2)}) %all-to-all-start) | async-done | bytes 1843232 | tf_op jit(solution)/shard_map/all_to_all | solution.py:15
  191.4 4.3 copy.17
  195.7 5.5 %reshape.69 = bf16[320,9,320]{2,0,1:T(8,128)(2,1)} reshape(bf16[64,5,9,320]{3,1,0,2:T(8,128)(2,1)} %copy.17) | data formatting | bytes 3686400 | tf_op jit(solution)/shard_map/reshape | solution.py:14
  201.2 0.0 copy-start.2
  201.2 1.5 fusion.32
  202.7 1.4 fusion.31
  204.2 0.0 copy-done.2
  204.2 0.4 convolution_add_fusion.6
  204.6 0.4 convolution_add_fusion.5
  205.0 0.5 convolution_add_fusion.4
  205.5 0.4 convolution_add_fusion.3
  206.0 0.4 convolution_add_fusion.2
  206.4 0.5 convolution_add_fusion.1
  206.9 1.2 fusion.8
  208.1 159.5 %reduce-scatter.3.cloned.1.call-done = f32[5,9,320]{2,1,0:T(8,128)} async-done(((f32[320,9,320]{2,1,0:T(8,128)}), f32[5,9,320]{2,1,0:T(8,128)}) %reduce-scatter.3.cloned.1.call-update) | async-done | bytes 57616 | tf_op jit(solution)/shard_map/reduce_scatter | solution.py:73
  367.5 54.7 %all-reduce.1 = f32[5,9,320]{2,1,0:T(8,128)S(1)} all-reduce(f32[5,9,320]{2,1,0:T(8,128)} %reduce-scatter.3.cloned.1.call-done), channel_id=3, replica_groups=mesh['band'=64,'strip'=8] {'strip'}, use_global_device_ids=true, to_apply=%region_1.2.clone | all-reduce | flops 14400 | bytes 115200
  422.2 0.1 dynamic-slice_multiply_fusion
  422.3 0.6 copy.20
Async XLA Ops:
  7.2 10.7 %copy-start = (bf16[1,320,6,128]{3,1,2,0:T(8,128)(2,1)S(1)}, bf16[1,320,6,128]{3,1,2,0:T(8,128)(2,1)}, u32[]{:S(2)}) copy-start(bf16[1,320,6,128]{3,1,2,0:T(8,128)(2,1)} %param.3) | copy-start | bytes 1474564
  7.2 12.0 %copy-start.1 = (bf16[1,320,6,128]{3,1,2,0:T(8,128)(2,1)S(1)}, bf16[1,320,6,128]{3,1,2,0:T(8,128)(2,1)}, u32[]{:S(2)}) copy-start(bf16[1,320,6,128]{3,1,2,0:T(8,128)(2,1)} %param.4) | copy-start | bytes 1474564
  7.2 360.4 %reduce-scatter.3.cloned.1.call-start = ((), (), s32[]{:S(2)}) async-start(), calls=%async_computation.2 | async-start | bytes 7987200 | tf_op jit(solution)/shard_map/reduce_scatter | solution.py:73
  8.3 6.3 %collective-permute-start.1 = (bf16[1,320,1,128]{3,1,2,0:T(8,128)(2,1)S(1)}, bf16[1,320,1,128]{3,1,2,0:T(8,128)(2,1)S(1)}, u32[]{:S(2)}, u32[]{:S(2)}) collective-permute-start(bf16[1,320,1,128]{3,1,2,0:T(8,128)(2,1)S(1)} %get-tuple-element.11), channel_id=1, source_target_pairs={{1,0},{2,1},{3,2},{4,3},{5,4},{6,5},{7,6},{9,8},{10,9},{11,10},{12... | collective-permute-start | bytes 245768 | tf_op jit(solution)/shard_map/ppermute | solution.py:32
  9.6 6.6 %collective-permute-start = (bf16[1,320,1,128]{3,1,2,0:T(8,128)(2,1)S(1)}, bf16[1,320,1,128]{3,1,2,0:T(8,128)(2,1)S(1)}, u32[]{:S(2)}, u32[]{:S(2)}) collective-permute-start(bf16[1,320,1,128]{3,1,2,0:T(8,128)(2,1)S(1)} %get-tuple-element.10), channel_id=1, source_target_pairs={{0,1},{1,2},{2,3},{3,4},{4,5},{5,6},{6,7},{8,9},{9,10},{10,11},{11... | collective-permute-start | bytes 245768 | tf_op jit(solution)/shard_map/ppermute | solution.py:30
  38.1 0.7 copy-start.3
  88.8 102.6 %all-to-all-start = ((bf16[64,5,9,320]{3,1,2,0:T(8,128)(2,1)}), bf16[64,5,9,320]{3,1,2,0:T(8,128)(2,1)}, u32[]{:S(2)}, u32[]{:S(2)}) async-start(bf16[64,5,9,320]{3,1,2,0:T(8,128)(2,1)} %stack.22), calls=%async_computation | async-start | bytes 7077888 | tf_op jit(solution)/shard_map/all_to_all | solution.py:15
  201.2 3.0 copy-start.2
Sparse Core Ops, SparseCore 0:
  38.3 329.2 reduce-scatter.2
